TPU v7x, 32 devices: a whole 2x2x4 slice. The times are simulated.
32 devices in a mesh: grp: 2 (over y), row: 4 (over z), col: 2 (over x), rep: 2 (over core).
Axes of the slice: x: 2, y: 2, z: 4, core: 2. Of those that a mesh axis runs over, the one named last changes fastest.
Arguments:
- shard_rows: bfloat16 [11520, 512], P(('grp', 'row', 'col', 'rep')), parts along dimension 0, may hold values from -24 to 24
- row_position: int32 [11520], P(('grp', 'row', 'col', 'rep')), parts along dimension 0, may hold values from 0 to 3071, as said below
- shard_count: int32 [32], P(('grp', 'row', 'col', 'rep')), parts along dimension 0, may hold values from 1 to 360, as said below
Outputs:
- max_similarity: float32 [6144], P(('grp', 'row', 'col', 'rep')), parts along dimension 0
There are 2 independent parts, one for each index of `grp`. A program takes and returns all parts, laid end to end along the dimension named above; each array names one. Nothing has to cross between parts.
Inputs may be any that keep to these rules, and one draw needn't show every extreme that they name: `row_position`: row j of shard s is used when j < shard_count[s]; the used rows of all shards hold every position 0 to 3071 once, unused rows hold arbitrary positions. At most 24 used rows of one shard have positions in one aligned run of 192 positions, and some shard reaches 24. `shard_count`: the counts sum to 3072.
All inputs are finite; a program needn't handle non-finite values.
Results may differ from a plain program's by a relative error of at most 0.00063.
Values may be sent and summed in bfloat16 or wider, within the bound.
A program may use at most 64 MiB of HBM per device.

v0:
```python
import math
import jax
import jax.numpy as jnp
from jax import lax
from jax.sharding import PartitionSpec as P

OWN = 192


def normalize(owned_rows):
    widened = owned_rows.astype(jnp.float32)
    return (widened / jnp.sqrt(jnp.sum(widened * widened, 1, keepdims=True) + 1e-06)).astype(
        jnp.bfloat16
    )


def body(shard_rows, row_position, shard_count):
    row_devices = lax.axis_size("row")
    cross_devices = lax.axis_size(("col", "rep"))
    all_shards = row_devices * cross_devices
    per_owner = OWN
    owner_load = max(1, per_owner // all_shards)
    slot_count = 2 * owner_load
    block_rows = per_owner * cross_devices
    capacity, feature = shard_rows.shape
    row_place = lax.axis_index("row")
    cross_place = lax.axis_index(("col", "rep"))
    is_used = jnp.arange(capacity) < shard_count[0]
    position = jnp.where(is_used, row_position, 0)
    owner_first = position // per_owner
    one_hot = jnp.logical_and(
        owner_first[:, None] == jnp.arange(all_shards)[None, :], is_used[:, None]
    ).astype(jnp.int32)
    ranking = jnp.sum(jnp.cumsum(one_hot, 0) * one_hot, 1) - 1
    target = jnp.where(is_used, owner_first * slot_count + ranking, all_shards * slot_count)
    packed = (
        jnp.zeros((all_shards * slot_count, feature), shard_rows.dtype)
        .at[target]
        .set(shard_rows, mode="drop")
    )
    placed = (
        jnp.full((all_shards * slot_count,), -1, jnp.int32).at[target].set(position, mode="drop")
    )
    first_packed = packed.reshape(row_devices, cross_devices, slot_count, feature)
    first_placed = placed.reshape(row_devices, cross_devices, slot_count)
    own_offset = row_place * block_rows + cross_place * per_owner
    received = (
        lax.all_to_all(
            lax.all_to_all(first_packed, "row", split_axis=0, concat_axis=0, tiled=True),
            ("col", "rep"),
            split_axis=1,
            concat_axis=1,
            tiled=True,
        ),
        lax.all_to_all(
            lax.all_to_all(first_placed, "row", split_axis=0, concat_axis=0, tiled=True),
            ("col", "rep"),
            split_axis=1,
            concat_axis=1,
            tiled=True,
        ),
    )
    flat_rows = received[0].reshape(-1, feature)
    flat_places = received[1].reshape(-1)
    local_index = jnp.where(flat_places >= 0, flat_places - own_offset, per_owner)
    owned_rows = (
        jnp.zeros((per_owner, feature), flat_rows.dtype).at[local_index].set(flat_rows, mode="drop")
    )
    row_owned = normalize(owned_rows)
    row_block = lax.all_gather(row_owned, ("col", "rep"), axis=0, tiled=True)
    column_index = jnp.arange(block_rows)
    column_block = lax.all_gather(row_owned, "row", axis=0, tiled=True)
    column_places = (
        column_index // per_owner * block_rows + cross_place * per_owner + column_index % per_owner
    )
    row_step = math.gcd(block_rows, 512)
    column_step = math.gcd(block_rows, 1024)

    def row_maxima(inputs):
        row_tile, row_start = inputs
        row_global = row_place * block_rows + row_start + jnp.arange(row_step)
        running = jnp.full((row_step,), -4.0, jnp.float32)
        for column_turn in range(block_rows // column_step):
            column_tile = column_block[column_turn * column_step : (column_turn + 1) * column_step]
            scores = jnp.einsum(
                "rd,cd->rc", row_tile, column_tile, preferred_element_type=jnp.float32
            )
            column_global = column_places[
                column_turn * column_step : (column_turn + 1) * column_step
            ]
            scores = jnp.where(row_global[:, None] == column_global[None, :], -4.0, scores)
            running = jnp.maximum(running, jnp.max(scores, 1))
        return running

    starts = jnp.arange(block_rows // row_step, dtype=jnp.int32) * row_step
    maxima = lax.map(row_maxima, (row_block.reshape(-1, row_step, feature), starts)).reshape(
        block_rows
    )
    combined = lax.pmax(maxima, ("col", "rep"))
    return lax.dynamic_slice_in_dim(combined, cross_place * per_owner, per_owner)


def solution(mesh):
    return jax.shard_map(
        body,
        mesh=mesh,
        in_specs=(
            P(("grp", "row", "col", "rep"), None),
            P(("grp", "row", "col", "rep")),
            P(("grp", "row", "col", "rep")),
        ),
        out_specs=P(("grp", "row", "col", "rep")),
        check_vma=False,
    )
```

profile of v0, /device:TPU:0, one launch (start us, length us, event | category | flops | bytes accessed | tf_op | source)
XLA Modules:
  0.0 92.6 jit_solution(1535740901777857113)
XLA Ops:
  0.7 0.7 copy-done
  1.4 0.9 reduce-window.6
  2.6 2.9 %scatter_custom_fusion = s32[384]{0:T(512)S(1)} fusion(s32[360]{0:T(512)S(1)} %compare_select_fusion.1, s32[360]{0:T(512)S(1)} %get-tuple-element.104, s32[]{:T(128)} %constant.84.clone.1), kind=kCustom, calls=%fused_computation.67 | custom fusion | bytes 1540 | tf_op jit(solution)/shard_map/scatter | solution.py:42
  5.5 0.7 reshape.115
  6.2 6.3 %all-to-all-start = ((s32[4,4,24]{2,1,0:T(4,128)}), s32[4,4,24]{2,1,0:T(4,128)S(1)}, u32[]{:S(2)}, u32[]{:S(2)}) async-start(s32[4,4,24]{2,1,0:T(4,128)} %reshape.115), calls=%async_computation | async-start | bytes 16384 | tf_op jit(solution)/shard_map/all_to_all | solution.py:56
  12.6 3.0 %scatter_custom_fusion.1 = bf16[384,512]{1,0:T(8,128)(2,1)} fusion(s32[360]{0:T(512)S(1)} %compare_select_fusion.1, bf16[360,512]{1,0:T(8,128)(2,1)} %param.5, bf16[]{:T(256)} %constant.83.clone.1), kind=kCustom, calls=%fused_computation.27 | custom fusion | bytes 393728 | tf_op jit(solution)/shard_map/scatter | solution.py:39
  15.6 2.6 %all-to-all-done = s32[4,4,24]{2,1,0:T(4,128)S(1)} async-done(((s32[4,4,24]{2,1,0:T(4,128)}), s32[4,4,24]{2,1,0:T(4,128)S(1)}, u32[]{:S(2)}, u32[]{:S(2)}) %all-to-all-start) | async-done | bytes 1568 | tf_op jit(solution)/shard_map/all_to_all | solution.py:56
  18.2 3.5 %all-to-all-start.2 = ((bf16[4,4,24,512]{3,2,1,0:T(8,128)(2,1)}), bf16[4,4,24,512]{3,2,1,0:T(8,128)(2,1)S(1)}, u32[]{:S(2)}, u32[]{:S(2)}) async-start(bf16[4,4,24,512]{3,2,1,0:T(8,128)(2,1)} %bitcast.5), calls=%async_computation.2 | async-start | bytes 786432 | tf_op jit(solution)/shard_map/all_to_all | solution.py:49
  21.6 0.6 copy.17
  22.2 9.9 %all-to-all-done.2 = bf16[4,4,24,512]{3,2,1,0:T(8,128)(2,1)S(1)} async-done(((bf16[4,4,24,512]{3,2,1,0:T(8,128)(2,1)}), bf16[4,4,24,512]{3,2,1,0:T(8,128)(2,1)S(1)}, u32[]{:S(2)}, u32[]{:S(2)}) %all-to-all-start.2) | async-done | bytes 393248 | tf_op jit(solution)/shard_map/all_to_all | solution.py:49
  32.1 3.2 %all-to-all-start.1 = ((s32[4,4,24]{2,0,1:T(4,128)}), s32[4,4,24]{2,0,1:T(4,128)S(1)}, u32[]{:S(2)}, u32[]{:S(2)}) async-start(s32[4,4,24]{2,0,1:T(4,128)} %copy.17), calls=%async_computation.1 | async-start | bytes 16384 | tf_op jit(solution)/shard_map/all_to_all | solution.py:55
  35.4 0.8 copy.19
  36.2 3.0 %all-to-all-done.1 = s32[4,4,24]{2,0,1:T(4,128)S(1)} async-done(((s32[4,4,24]{2,0,1:T(4,128)}), s32[4,4,24]{2,0,1:T(4,128)S(1)}, u32[]{:S(2)}, u32[]{:S(2)}) %all-to-all-start.1) | async-done | bytes 1568 | tf_op jit(solution)/shard_map/all_to_all | solution.py:55
  39.1 3.5 %all-to-all-start.3 = ((bf16[4,4,24,512]{3,2,0,1:T(8,128)(2,1)}), bf16[4,4,24,512]{3,2,0,1:T(8,128)(2,1)S(1)}, u32[]{:S(2)}, u32[]{:S(2)}) async-start(bf16[4,4,24,512]{3,2,0,1:T(8,128)(2,1)} %copy.19), calls=%async_computation.3 | async-start | bytes 786432 | tf_op jit(solution)/shard_map/all_to_all | solution.py:48
  42.7 7.3 %all-to-all-done.3 = bf16[4,4,24,512]{3,2,0,1:T(8,128)(2,1)S(1)} async-done(((bf16[4,4,24,512]{3,2,0,1:T(8,128)(2,1)}), bf16[4,4,24,512]{3,2,0,1:T(8,128)(2,1)S(1)}, u32[]{:S(2)}, u32[]{:S(2)}) %all-to-all-start.3) | async-done | bytes 393248 | tf_op jit(solution)/shard_map/all_to_all | solution.py:48
  50.0 2.0 %scatter_custom_fusion.2 = bf16[192,512]{1,0:T(8,128)(2,1)S(1)} fusion(s32[384]{0:T(512)S(1)} %fusion.35, bf16[384,512]{1,0:T(8,128)(2,1)S(1)} %bitcast.40, bf16[]{:T(256)} %constant.83.clone.1), kind=kCustom, calls=%fused_computation.29 | custom fusion | bytes 196610 | tf_op jit(solution)/shard_map/scatter | solution.py:67
  52.3 18.0 %all_gather.7 = bf16[768,512]{1,0:T(8,128)(2,1)S(1)} all-gather(bf16[192,512]{1,0:T(8,128)(2,1)S(1)} %fusion.16), channel_id=1, replica_groups=mesh['grp'=2,'row'=4,'col'=2,'rep'=2] {'row'}, dimensions={0}, use_global_device_ids=true | all-gather | bytes 983040 | tf_op jit(solution)/shard_map/all_gather | solution.py:72
  70.3 7.5 %all_gather.6 = bf16[768,512]{1,0:T(8,128)(2,1)S(1)} all-gather(bf16[192,512]{1,0:T(8,128)(2,1)S(1)} %fusion.16), channel_id=1, replica_groups=mesh['grp'=2,'row'=4,'col'=2,'rep'=2] {'col','rep'}, dimensions={0}, use_global_device_ids=true | all-gather | bytes 983040 | tf_op jit(solution)/shard_map/all_gather | solution.py:70
  77.8 6.9 %while.12 = (s32[]{:T(128)}, f32[3,256]{1,0:T(4,128)S(1)}, s32[3]{0:T(128)S(1)}, s32[]{:T(128)}, s32[768]{0:T(1024)S(1)}, /*index=5*/bf16[3,256,512]{2,1,0:T(8,1...) while((s32[]{:T(128)}, f32[3,256]{1,0:T(4,128)S(1)}, s32[3]{0:T(128)S(1)}, s32[]{:T(128)}, ...), condition=%wide.region_11.12_spmd, body=%wide.region_7.11_spmd.sunk | while | flops 201916672 | bytes 1595529 | solution.py:96
  77.8 0.7 dynamic_slice.35
  79.1 0.3 fusion.58
  79.4 0.3 fusion.57
  79.7 0.3 fusion.56
  80.1 0.7 dynamic_slice.35
  81.4 0.3 fusion.58
  81.7 0.3 fusion.57
  82.0 0.3 fusion.56
  82.3 0.7 dynamic_slice.35
  83.7 0.3 fusion.58
  84.3 0.3 fusion.56
  84.6 7.3 %pmax.7 = f32[768]{0:T(1024)S(1)} all-reduce(f32[768]{0:T(1024)S(1)} %reshape.119), channel_id=1, replica_groups=mesh['grp'=2,'row'=4,'col'=2,'rep'=2] {'col','rep'}, use_global_device_ids=true, to_apply=%region_12.13 | all-reduce | flops 768 | bytes 6144 | tf_op jit(solution)/shard_map/pmax | solution.py:99
  91.9 0.6 dynamic_slice.15
  (32 shorter events, 1.3 us)
Async XLA Ops:
  0.7 0.7 copy-start
  6.2 11.9 %all-to-all-start = ((s32[4,4,24]{2,1,0:T(4,128)}), s32[4,4,24]{2,1,0:T(4,128)S(1)}, u32[]{:S(2)}, u32[]{:S(2)}) async-start(s32[4,4,24]{2,1,0:T(4,128)} %reshape.115), calls=%async_computation | async-start | bytes 16384 | tf_op jit(solution)/shard_map/all_to_all | solution.py:56
  18.2 14.0 %all-to-all-start.2 = ((bf16[4,4,24,512]{3,2,1,0:T(8,128)(2,1)}), bf16[4,4,24,512]{3,2,1,0:T(8,128)(2,1)S(1)}, u32[]{:S(2)}, u32[]{:S(2)}) async-start(bf16[4,4,24,512]{3,2,1,0:T(8,128)(2,1)} %bitcast.5), calls=%async_computation.2 | async-start | bytes 786432 | tf_op jit(solution)/shard_map/all_to_all | solution.py:49
  32.1 7.0 %all-to-all-start.1 = ((s32[4,4,24]{2,0,1:T(4,128)}), s32[4,4,24]{2,0,1:T(4,128)S(1)}, u32[]{:S(2)}, u32[]{:S(2)}) async-start(s32[4,4,24]{2,0,1:T(4,128)} %copy.17), calls=%async_computation.1 | async-start | bytes 16384 | tf_op jit(solution)/shard_map/all_to_all | solution.py:55
  39.1 10.9 %all-to-all-start.3 = ((bf16[4,4,24,512]{3,2,0,1:T(8,128)(2,1)}), bf16[4,4,24,512]{3,2,0,1:T(8,128)(2,1)S(1)}, u32[]{:S(2)}, u32[]{:S(2)}) async-start(bf16[4,4,24,512]{3,2,0,1:T(8,128)(2,1)} %copy.19), calls=%async_computation.3 | async-start | bytes 786432 | tf_op jit(solution)/shard_map/all_to_all | solution.py:48
where the time goes:
time: 93.1 us; the launch traced here: 92.6 us
  blocking collectives  32.8 us (35%)
  waiting for transfers between devices  22.7 us (24%)
  starting transfers between devices  16.5 us (18%)
  local copies, waits for them, and re-layouts  13.7 us (15%)
  matrix products  2.53 us (3%)
  loops' own time  2.18 us (2%)
  other arithmetic  1.38 us (1%)
    all_gather x1, blocking collectives, body(): column_block = lax.all_gather(row_owned, 'row', axis=0, tiled=True)  18 us
    all_to_all x1, waiting for transfers between devices, body(): lax.all_to_all(first_packed, 'row', split_axis=0, concat_axis=0, tiled=True)  9.87 us
    all_gather x1, blocking collectives, body(): row_block = lax.all_gather(row_owned, ('col', 'rep'), axis=0, tiled=True)  7.46 us
    pmax x1, blocking collectives, body(): combined = lax.pmax(maxima, ('col', 'rep'))  7.28 us
    all_to_all x1, waiting for transfers between devices, body(): lax.all_to_all(lax.all_to_all(first_packed, 'row', split_axis=0, concat_a...  7.27 us
    all_to_all x1, starting transfers between devices, body(): lax.all_to_all(first_placed, 'row', split_axis=0, concat_axis=0, tiled=True)  6.32 us
    all_to_all x1, starting transfers between devices, body(): lax.all_to_all(lax.all_to_all(first_packed, 'row', split_axis=0, concat_a...  3.46 us
    all_to_all x1, starting transfers between devices, body(): lax.all_to_all(first_packed, 'row', split_axis=0, concat_axis=0, tiled=True)  3.46 us
  transfers between devices with their start and end apart: 4, of which 4 were waited for; matrix products, arithmetic and copies ran while one was open for 5% of the time, Pallas kernels for 0%

commit v1 on v0

--- a/solution.py
+++ b/solution.py
@@ -5,6 +5,22 @@
 from jax.sharding import PartitionSpec as P
 
 OWN = 192
+
+
+def roots_check(v0):
+    k_all = lax.axis_size("row")
+    tile_out = sorted(((pp, (pp + 1) % k_all) for pp in range(k_all)))
+    r_now = v0
+    rack = [r_now]
+    dev_j = 1
+    while dev_j < k_all:
+        r_now = lax.ppermute(r_now, "row", tile_out)
+        rack.insert(0, r_now)
+        dev_j += 1
+    r2 = jnp.concatenate(rack, axis=0)
+    r1 = lax.axis_index("row")
+    current_value = r1 + 1
+    return jnp.roll(r2, current_value * v0.shape[0], axis=0)
 
 
 def normalize(owned_rows):
@@ -69,7 +85,7 @@
     row_owned = normalize(owned_rows)
     row_block = lax.all_gather(row_owned, ("col", "rep"), axis=0, tiled=True)
     column_index = jnp.arange(block_rows)
-    column_block = lax.all_gather(row_owned, "row", axis=0, tiled=True)
+    column_block = roots_check(row_owned)
     column_places = (
         column_index // per_owner * block_rows + cross_place * per_owner + column_index % per_owner
     )

time: 93.1 us -> 91.4 us (0.982)
  blocking collectives: 32.8 us -> 14.7 us
  waiting for transfers between devices: 22.7 us -> 38.4 us
    all_gather x1 -> x0, blocking collectives: 18 us -> none  [body(): column_block = lax.all_gather(row_owned, 'row', axis=0, tiled=True)]
    ppermute x0 -> x3, waiting for transfers between devices: none -> 15.6 us  [roots_check(): r_now = lax.ppermute(r_now, 'row', tile_out)]
  transfers between devices with their start and end apart: 4 -> 7, of which waited for: 4 -> 6; matrix products, arithmetic and copies ran while one was open for 5% -> 5% of each run, Pallas kernels for 0% -> 0%
where the time goes in v1:
time: 91.4 us; the launch traced here: 90.9 us
  waiting for transfers between devices  38.4 us (42%)
  starting transfers between devices  16.5 us (18%)
  blocking collectives  14.7 us (16%)
  local copies, waits for them, and re-layouts  13.4 us (15%)
  matrix products  2.53 us (3%)
  other arithmetic  2.27 us (2%)
  loops' own time  2.2 us (2%)
    ppermute x3, waiting for transfers between devices, roots_check(): r_now = lax.ppermute(r_now, 'row', tile_out)  15.6 us
    all_to_all x1, waiting for transfers between devices, body(): lax.all_to_all(first_packed, 'row', split_axis=0, concat_axis=0, tiled=True)  9.9 us
    all_gather x1, blocking collectives, body(): row_block = lax.all_gather(row_owned, ('col', 'rep'), axis=0, tiled=True)  7.9 us
    all_to_all x1, waiting for transfers between devices, body(): lax.all_to_all(lax.all_to_all(first_packed, 'row', split_axis=0, concat_a...  7.26 us
    pmax x1, blocking collectives, body(): combined = lax.pmax(maxima, ('col', 'rep'))  6.83 us
    all_to_all x1, starting transfers between devices, body(): lax.all_to_all(first_placed, 'row', split_axis=0, concat_axis=0, tiled=True)  6.32 us
    all_to_all x1, starting transfers between devices, body(): lax.all_to_all(first_packed, 'row', split_axis=0, concat_axis=0, tiled=True)  3.46 us
    all_to_all x1, starting transfers between devices, body(): lax.all_to_all(lax.all_to_all(first_packed, 'row', split_axis=0, concat_a...  3.46 us
  transfers between devices with their start and end apart: 7, of which 6 were waited for; matrix products, arithmetic and copies ran while one was open for 5% of the time, Pallas kernels for 0%

profile of v1, /device:TPU:0, one launch (start us, length us, event | category | flops | bytes accessed | tf_op | source)
XLA Modules:
  0.0 90.9 jit_solution(8878363650220780315)
XLA Ops:
  0.7 0.7 add_select_fusion.1
  1.4 0.9 reduce-window.6
  2.6 2.9 %scatter_custom_fusion = s32[384]{0:T(512)S(1)} fusion(s32[360]{0:T(512)S(1)} %compare_select_fusion.1, s32[360]{0:T(512)S(1)} %get-tuple-element.104, s32[]{:T(128)} %constant.101.clone.1), kind=kCustom, calls=%fused_computation.75 | custom fusion | bytes 1540 | tf_op jit(solution)/shard_map/scatter | solution.py:58
  5.6 0.7 reshape.115
  6.3 6.3 %all-to-all-start = ((s32[4,4,24]{2,1,0:T(4,128)}), s32[4,4,24]{2,1,0:T(4,128)S(1)}, u32[]{:S(2)}, u32[]{:S(2)}) async-start(s32[4,4,24]{2,1,0:T(4,128)} %reshape.115), calls=%async_computation | async-start | bytes 16384 | tf_op jit(solution)/shard_map/all_to_all | solution.py:72
  12.6 3.0 %scatter_custom_fusion.1 = bf16[384,512]{1,0:T(8,128)(2,1)} fusion(s32[360]{0:T(512)S(1)} %compare_select_fusion.1, bf16[360,512]{1,0:T(8,128)(2,1)} %param.5, bf16[]{:T(256)} %constant.100.clone.1), kind=kCustom, calls=%fused_computation.27 | custom fusion | bytes 393728 | tf_op jit(solution)/shard_map/scatter | solution.py:55
  15.6 2.6 %all-to-all-done = s32[4,4,24]{2,1,0:T(4,128)S(1)} async-done(((s32[4,4,24]{2,1,0:T(4,128)}), s32[4,4,24]{2,1,0:T(4,128)S(1)}, u32[]{:S(2)}, u32[]{:S(2)}) %all-to-all-start) | async-done | bytes 1568 | tf_op jit(solution)/shard_map/all_to_all | solution.py:72
  18.2 3.5 %all-to-all-start.2 = ((bf16[4,4,24,512]{3,2,1,0:T(8,128)(2,1)}), bf16[4,4,24,512]{3,2,1,0:T(8,128)(2,1)S(1)}, u32[]{:S(2)}, u32[]{:S(2)}) async-start(bf16[4,4,24,512]{3,2,1,0:T(8,128)(2,1)} %bitcast.5), calls=%async_computation.2 | async-start | bytes 786432 | tf_op jit(solution)/shard_map/all_to_all | solution.py:65
  21.6 0.6 copy.17
  22.2 9.9 %all-to-all-done.2 = bf16[4,4,24,512]{3,2,1,0:T(8,128)(2,1)S(1)} async-done(((bf16[4,4,24,512]{3,2,1,0:T(8,128)(2,1)}), bf16[4,4,24,512]{3,2,1,0:T(8,128)(2,1)S(1)}, u32[]{:S(2)}, u32[]{:S(2)}) %all-to-all-start.2) | async-done | bytes 393248 | tf_op jit(solution)/shard_map/all_to_all | solution.py:65
  32.1 3.2 %all-to-all-start.1 = ((s32[4,4,24]{2,0,1:T(4,128)}), s32[4,4,24]{2,0,1:T(4,128)S(1)}, u32[]{:S(2)}, u32[]{:S(2)}) async-start(s32[4,4,24]{2,0,1:T(4,128)} %copy.17), calls=%async_computation.1 | async-start | bytes 16384 | tf_op jit(solution)/shard_map/all_to_all | solution.py:71
  35.4 0.8 copy.19
  36.2 3.0 %all-to-all-done.1 = s32[4,4,24]{2,0,1:T(4,128)S(1)} async-done(((s32[4,4,24]{2,0,1:T(4,128)}), s32[4,4,24]{2,0,1:T(4,128)S(1)}, u32[]{:S(2)}, u32[]{:S(2)}) %all-to-all-start.1) | async-done | bytes 1568 | tf_op jit(solution)/shard_map/all_to_all | solution.py:71
  39.1 3.5 %all-to-all-start.3 = ((bf16[4,4,24,512]{3,2,0,1:T(8,128)(2,1)}), bf16[4,4,24,512]{3,2,0,1:T(8,128)(2,1)S(1)}, u32[]{:S(2)}, u32[]{:S(2)}) async-start(bf16[4,4,24,512]{3,2,0,1:T(8,128)(2,1)} %copy.19), calls=%async_computation.3 | async-start | bytes 786432 | tf_op jit(solution)/shard_map/all_to_all | solution.py:64
  42.8 7.3 %all-to-all-done.3 = bf16[4,4,24,512]{3,2,0,1:T(8,128)(2,1)S(1)} async-done(((bf16[4,4,24,512]{3,2,0,1:T(8,128)(2,1)}), bf16[4,4,24,512]{3,2,0,1:T(8,128)(2,1)S(1)}, u32[]{:S(2)}, u32[]{:S(2)}) %all-to-all-start.3) | async-done | bytes 393248 | tf_op jit(solution)/shard_map/all_to_all | solution.py:64
  50.1 2.0 %scatter_custom_fusion.2 = bf16[192,512]{1,0:T(8,128)(2,1)S(1)} fusion(s32[384]{0:T(512)S(1)} %fusion.35, bf16[384,512]{1,0:T(8,128)(2,1)S(1)} %bitcast.40, bf16[]{:T(256)} %constant.100.clone.1), kind=kCustom, calls=%fused_computation.29 | custom fusion | bytes 196610 | tf_op jit(solution)/shard_map/scatter | solution.py:83
  52.4 8.2 %collective-permute-done = bf16[192,512]{1,0:T(8,128)(2,1)S(1)} collective-permute-done((bf16[192,512]{1,0:T(8,128)(2,1)S(1)}, bf16[192,512]{1,0:T(8,128)(2,1)S(1)}, u32[]{:S(2)}, u32[]{:S(2)}) %collective-permute-start) | collective-permute-done | bytes 196640 | tf_op jit(solution)/shard_map/ppermute | solution.py:17
  60.6 7.4 %collective-permute-done.1 = bf16[192,512]{1,0:T(8,128)(2,1)S(1)} collective-permute-done((bf16[192,512]{1,0:T(8,128)(2,1)S(1)}, bf16[192,512]{1,0:T(8,128)(2,1)S(1)}, u32[]{:S(2)}, u32[]{:S(2)}) %collective-permute-start.1) | collective-permute-done | bytes 196640 | tf_op jit(solution)/shard_map/ppermute | solution.py:17
  68.1 7.9 %all_gather.3 = bf16[768,512]{1,0:T(8,128)(2,1)S(1)} all-gather(bf16[192,512]{1,0:T(8,128)(2,1)S(1)} %fusion.16), channel_id=1, replica_groups=mesh['grp'=2,'row'=4,'col'=2,'rep'=2] {'col','rep'}, dimensions={0}, use_global_device_ids=true | all-gather | bytes 983040 | tf_op jit(solution)/shard_map/all_gather | solution.py:86
  76.5 6.9 %while.12 = (s32[]{:T(128)}, f32[3,256]{1,0:T(4,128)S(1)}, s32[3]{0:T(128)S(1)}, s32[]{:T(128)}, s32[768]{0:T(1024)S(1)}, /*index=5*/bf16[3,256,512]{2,1,0:T(8,1...) while((s32[]{:T(128)}, f32[3,256]{1,0:T(4,128)S(1)}, s32[3]{0:T(128)S(1)}, s32[]{:T(128)}, ...), condition=%wide.region_11.12_spmd, body=%wide.region_7.11_spmd.sunk | while | flops 201916672 | bytes 1595529 | solution.py:112
  76.5 0.7 dynamic_slice.41
  77.9 0.3 fusion.58
  78.2 0.3 fusion.57
  78.5 0.3 fusion.56
  78.8 0.7 dynamic_slice.41
  80.2 0.3 fusion.58
  80.8 0.3 fusion.56
  81.1 0.7 dynamic_slice.41
  82.5 0.3 fusion.58
  83.1 0.3 fusion.56
  83.4 6.8 %pmax.7 = f32[768]{0:T(1024)S(1)} all-reduce(f32[768]{0:T(1024)S(1)} %reshape.119), channel_id=1, replica_groups=mesh['grp'=2,'row'=4,'col'=2,'rep'=2] {'col','rep'}, use_global_device_ids=true, to_apply=%region_12.13 | all-reduce | flops 768 | bytes 6144 | tf_op jit(solution)/shard_map/pmax | solution.py:115
  90.3 0.6 dynamic_slice.20
  (44 shorter events, 2.1 us)
Async XLA Ops:
  6.3 11.9 %all-to-all-start = ((s32[4,4,24]{2,1,0:T(4,128)}), s32[4,4,24]{2,1,0:T(4,128)S(1)}, u32[]{:S(2)}, u32[]{:S(2)}) async-start(s32[4,4,24]{2,1,0:T(4,128)} %reshape.115), calls=%async_computation | async-start | bytes 16384 | tf_op jit(solution)/shard_map/all_to_all | solution.py:72
  18.2 14.0 %all-to-all-start.2 = ((bf16[4,4,24,512]{3,2,1,0:T(8,128)(2,1)}), bf16[4,4,24,512]{3,2,1,0:T(8,128)(2,1)S(1)}, u32[]{:S(2)}, u32[]{:S(2)}) async-start(bf16[4,4,24,512]{3,2,1,0:T(8,128)(2,1)} %bitcast.5), calls=%async_computation.2 | async-start | bytes 786432 | tf_op jit(solution)/shard_map/all_to_all | solution.py:65
  32.1 7.0 %all-to-all-start.1 = ((s32[4,4,24]{2,0,1:T(4,128)}), s32[4,4,24]{2,0,1:T(4,128)S(1)}, u32[]{:S(2)}, u32[]{:S(2)}) async-start(s32[4,4,24]{2,0,1:T(4,128)} %copy.17), calls=%async_computation.1 | async-start | bytes 16384 | tf_op jit(solution)/shard_map/all_to_all | solution.py:71
  39.1 10.9 %all-to-all-start.3 = ((bf16[4,4,24,512]{3,2,0,1:T(8,128)(2,1)}), bf16[4,4,24,512]{3,2,0,1:T(8,128)(2,1)S(1)}, u32[]{:S(2)}, u32[]{:S(2)}) async-start(bf16[4,4,24,512]{3,2,0,1:T(8,128)(2,1)} %copy.19), calls=%async_computation.3 | async-start | bytes 786432 | tf_op jit(solution)/shard_map/all_to_all | solution.py:64
  52.3 8.3 %collective-permute-start = (bf16[192,512]{1,0:T(8,128)(2,1)S(1)}, bf16[192,512]{1,0:T(8,128)(2,1)S(1)}, u32[]{:S(2)}, u32[]{:S(2)}) collective-permute-start(bf16[192,512]{1,0:T(8,128)(2,1)S(1)} %fusion.16), channel_id=1, source_target_pairs={{0,4},{4,8},{8,12},{12,0},{1,5},{5,9},{9,13},{13,1},{2,6},{6,10},{... | collective-permute-start | bytes 589832 | tf_op jit(solution)/shard_map/ppermute | solution.py:17
  60.6 7.5 %collective-permute-start.1 = (bf16[192,512]{1,0:T(8,128)(2,1)S(1)}, bf16[192,512]{1,0:T(8,128)(2,1)S(1)}, u32[]{:S(2)}, u32[]{:S(2)}) collective-permute-start(bf16[192,512]{1,0:T(8,128)(2,1)S(1)} %collective-permute-done), channel_id=1, source_target_pairs={{0,4},{4,8},{8,12},{12,0},{1,5},{5,9},{9,13},{13,1},{2,6},{6,10},{... | collective-permute-start | bytes 589832 | tf_op jit(solution)/shard_map/ppermute | solution.py:17
  68.0 7.9 %collective-permute-start.2 = (bf16[192,512]{1,0:T(8,128)(2,1)S(1)}, bf16[192,512]{1,0:T(8,128)(2,1)S(1)}, u32[]{:S(2)}, u32[]{:S(2)}) collective-permute-start(bf16[192,512]{1,0:T(8,128)(2,1)S(1)} %collective-permute-done.1), channel_id=1, source_target_pairs={{0,4},{4,8},{8,12},{12,0},{1,5},{5,9},{9,13},{13,1},{2,6},{6,10},{... | collective-permute-start | bytes 589832 | tf_op jit(solution)/shard_map/ppermute | solution.py:17
